TPU v7x, 128 devices: a whole 4x4x4 slice. The times are simulated.
128 devices in a mesh: row: 8 (over y_lo, z), col: 16 (over y_hi, x, core).
Axes of the slice: x: 4, y: 4 (y_hi: 2, y_lo: 2; y = y_hi * 2 + y_lo), z: 4, core: 2. Of those that a mesh axis runs over, the one named last changes fastest.
Arguments:
- features: bfloat16 [24576, 512], P(('col', 'row')), may hold values from -6 to 6
- out_grad: bfloat16 [24576, 512], P(('row', 'col')), may hold values from -6 to 6
- weight: bfloat16 [512, 512], replicated, may hold values from -0.25 to 0.25
- block_values: bfloat16 [8, 16, 288, 4096], P('row', 'col'), may hold values from -0.125 to 0.125
- block_coords: int32 [8, 16, 2, 288], P('row', 'col'), may hold values from 0 to 47, as said below
- block_counts: int32 [8, 16], P('row', 'col'), may hold values from 1 to 288, as said below
Outputs:
- activations: bfloat16 [24576, 512], P(('row', 'col'))
- weight_grad: float32 [512, 512], replicated
- feature_grad: bfloat16 [24576, 512], P(('col', 'row'))
Inputs may be any that keep to these rules, and one draw needn't show every extreme that they name: `block_coords`: entry 0 of a slot is a block row below 48, entry 1 a block column below 24; the 288 slots of a tile name distinct blocks. `block_counts`: slots from the count onward are padding: their coordinates and values are ignored. Some tile has exactly 288 live slots.
All inputs are finite; a program needn't handle non-finite values.
Results may differ from a plain program's by a relative error of at most 0.025.
Values may be sent and summed in bfloat16 or wider, within the bound.
No kernel may reach another device: no remote copies, remote signals or barrier semaphores. Data moves between devices by JAX's collectives and lax.ppermute only.
A program may use at most 128 MiB of HBM per device.

v0:
```python
import math
import jax
import jax.numpy as jnp
from jax import lax
from jax.sharding import PartitionSpec as P


def settle(term):
    return lax.optimization_barrier(term.astype(jnp.bfloat16)).astype(jnp.float32)


def per_device(features, out_grad, weight, block_values, block_coords, block_counts):
    row_devices = lax.axis_size("row")
    col_devices = lax.axis_size("col")
    node_count = features.shape[0]
    side = 64
    slot_total = block_values.shape[2]
    block_rows = node_count * col_devices // side
    block_cols = node_count * row_devices // side
    live_count = block_counts[0, 0]
    row_ids = block_coords[0, 0, 0]
    col_ids = block_coords[0, 0, 1]
    slot_vals = block_values.reshape(slot_total, side, side)
    live = jnp.arange(slot_total, dtype=jnp.int32) < live_count
    slot_vals = jnp.where(live[:, None, None], slot_vals, jnp.zeros_like(slot_vals))
    panel = lax.all_gather(features, "row", axis=0, tiled=True)
    dense_tile = jnp.zeros((block_rows, side, block_cols, side), jnp.bfloat16)
    dense_tile = dense_tile.at[row_ids, :, col_ids, :].add(slot_vals)
    dense_tile = dense_tile.reshape(block_rows * side, block_cols * side)
    partial_agg = settle(jnp.dot(dense_tile, panel, preferred_element_type=jnp.float32))
    aggregated = lax.psum_scatter(
        partial_agg.astype(jnp.bfloat16), "col", scatter_dimension=0, tiled=True
    )
    pre_act = jnp.dot(aggregated, weight, preferred_element_type=jnp.float32)
    sigmoid_pre = jax.nn.sigmoid(pre_act)
    activations = (pre_act * sigmoid_pre).astype(jnp.bfloat16)
    grad_pre = (
        out_grad.astype(jnp.float32) * sigmoid_pre * (1.0 + pre_act * (1.0 - sigmoid_pre))
    ).astype(jnp.bfloat16)
    activations, grad_pre = (activations, grad_pre)
    grad_agg = lax.dot_general(
        grad_pre, weight, (((1,), (1,)), ((), ())), preferred_element_type=jnp.float32
    ).astype(jnp.bfloat16)
    grad_rows = lax.all_gather(grad_agg, "col", axis=0, tiled=True)
    local_wgrad = lax.dot_general(
        aggregated, grad_pre, (((0,), (0,)), ((), ())), preferred_element_type=jnp.float32
    )
    total_nodes = node_count * row_devices * col_devices
    weight_grad = lax.psum(local_wgrad, ("row", "col")) * jnp.float32(1.0 / math.sqrt(total_nodes))
    partial_grad = settle(
        lax.dot_general(
            dense_tile, grad_rows, (((0,), (0,)), ((), ())), preferred_element_type=jnp.float32
        )
    )
    feature_grad = lax.psum_scatter(
        partial_grad.astype(jnp.bfloat16), "row", scatter_dimension=0, tiled=True
    )
    return (activations, weight_grad, feature_grad)


def solution(mesh):
    return jax.shard_map(
        per_device,
        mesh=mesh,
        in_specs=(
            P(("col", "row"), None),
            P(("row", "col"), None),
            P(),
            P("row", "col", None, None),
            P("row", "col", None, None),
            P("row", "col"),
        ),
        out_specs=(P(("row", "col"), None), P(), P(("col", "row"), None)),
        check_vma=False,
    )
```

profile of v0, /device:TPU:0, one launch (start us, length us, event | category | flops | bytes accessed | tf_op | source)
XLA Modules:
  0.0 468.9 jit_solution(1539356239016432633)
XLA Ops:
  7.2 0.0 copy-start
  7.2 0.0 all-gather.3.cloned.1.call-start
  7.2 0.7 all-gather.3.cloned.1.call-update
  7.9 0.0 reduce-scatter.3.cloned.1.call-start
  8.0 4.5 copy.9
  13.1 3.9 broadcast_select_fusion
  17.0 0.0 copy-start.1
  17.0 9.9 %copy.10 = bf16[288,64,64]{2,1,0:T(8,128)(2,1)} copy(bf16[288,64,64]{0,2,1:T(8,128)(2,1)} %broadcast_select_fusion) | data formatting | bytes 4718592 | tf_op jit(solution)/shard_map/jit(_where)/select_n | solution.py:25
  26.9 0.0 copy-done.1
  26.9 7.1 %broadcast_in_dim.17 = bf16[48,64,24,64]{3,1,2,0:T(8,128)(2,1)} broadcast(bf16[]{:T(256)} %constant.6.clone.1), dimensions={} | broadcast | bytes 9437186 | tf_op jit(solution)/shard_map/broadcast_in_dim | solution.py:27
  34.0 45.5 %scatter_fusion = bf16[48,64,24,64]{3,1,2,0:T(8,128)(2,1)} fusion(bf16[48,64,24,64]{3,1,2,0:T(8,128)(2,1)} %broadcast_in_dim.17, s32[288]{0:T(512)S(1)} %fusion.1, bf16[288,64,64]{2,1,0:T(8,128)(2,1)} %copy.10), kind=kCustom, calls=%fused_computation | custom fusion | flops 1179648 | bytes 7080192 | tf_op jit(solution)/shard_map/scatter-add | solution.py:28
  79.6 22.7 %copy.11 = bf16[48,64,24,64]{3,2,1,0:T(8,128)(2,1)} copy(bf16[48,64,24,64]{3,1,2,0:T(8,128)(2,1)} %scatter_fusion) | data formatting | bytes 18874368 | tf_op jit(solution)/shard_map/scatter-add | solution.py:28
  102.2 24.6 %reshape.73 = bf16[3072,1536]{1,0:T(8,128)(2,1)} reshape(bf16[48,64,24,64]{3,2,1,0:T(8,128)(2,1)} %copy.11) | data formatting | bytes 18874368 | tf_op jit(solution)/shard_map/reshape | solution.py:29
  126.8 0.0 all-gather.3.cloned.1.call-done
  126.8 9.2 %convolution_convert_fusion = bf16[3072,512]{1,0:T(8,128)(2,1)} fusion(bf16[3072,1536]{1,0:T(8,128)(2,1)} %reshape.73, bf16[1536,512]{1,0:T(8,128)(2,1)} %all-gather.3.cloned.1.call-done), kind=kOutput, calls=%fused_computation.1 | convolution fusion | flops 4833411072 | bytes 14155776 | tf_op jit(solution)/shard_map/dot_general | solution.py:30
  136.1 0.0 copy-start.2
  136.1 0.0 reduce-scatter.3.cloned.1.call-update
  136.1 0.0 all-gather.5.cloned.1.call-start
  136.1 77.8 %reduce-scatter.3.cloned.1.call-done = bf16[192,512]{1,0:T(8,128)(2,1)} async-done(((bf16[3072,512]{1,0:T(8,128)(2,1)}), bf16[192,512]{1,0:T(8,128)(2,1)}) %reduce-scatter.3.cloned.1.call-update) | async-done | bytes 196624 | tf_op jit(solution)/shard_map/reduce_scatter | solution.py:31
  213.9 0.0 copy-done
  213.9 0.0 copy-start.3
  213.9 2.0 multiply_convert_fusion.1
  216.0 0.0 copy-done.2
  216.0 1.0 convolution_convert_fusion.2
  217.0 0.0 all-gather.5.cloned.1.call-update
  217.0 0.0 all-reduce.2.cloned.1.call-start
  217.1 0.0 copy-done.3
  217.1 1.4 fusion.2
  218.5 0.0 all-reduce.2.cloned.1.call-update
  218.5 0.2 reduce-scatter.5.cloned.1.call-start
  218.7 49.6 %all-gather.5.cloned.1.call-done = bf16[3072,512]{1,0:T(8,128)(2,1)} async-done(((bf16[192,512]{1,0:T(8,128)(2,1)}), bf16[3072,512]{1,0:T(8,128)(2,1)}) %all-gather.5.cloned.1.call-update) | async-done | bytes 3145744 | tf_op jit(solution)/shard_map/all_gather | solution.py:44
  268.3 10.4 %convolution_convert_fusion.1 = bf16[1536,512]{1,0:T(8,128)(2,1)} fusion(bf16[3072,1536]{1,0:T(8,128)(2,1)} %reshape.73, bf16[3072,512]{1,0:T(8,128)(2,1)} %all-gather.5.cloned.1.call-done), kind=kOutput, calls=%fused_computation.3 | convolution fusion | flops 4832624640 | bytes 14155776 | tf_op jit(solution)/shard_map/dot_general | solution.py:51
  278.7 0.0 reduce-scatter.5.cloned.1.call-update
  278.7 140.3 %all-reduce.2.cloned.1.call-done = f32[512,512]{1,0:T(8,128)} async-done(((f32[512,512]{1,0:T(8,128)}), f32[512,512]{1,0:T(8,128)}) %all-reduce.2.cloned.1.call-update) | async-done | bytes 1048592 | tf_op jit(solution)/shard_map/psum | solution.py:49
  419.0 2.3 broadcast_multiply_fusion
  421.3 41.0 %reduce-scatter.5.cloned.1.call-done = bf16[192,512]{1,0:T(8,128)(2,1)} async-done(((bf16[1536,512]{1,0:T(8,128)(2,1)}), bf16[192,512]{1,0:T(8,128)(2,1)}) %reduce-scatter.5.cloned.1.call-update) | async-done | bytes 196624 | tf_op jit(solution)/shard_map/reduce_scatter | solution.py:55
  (2 shorter events, 0.0 us)
Async XLA Ops:
  7.2 206.8 %copy-start = (bf16[512,512]{1,0:T(8,128)(2,1)S(1)}, bf16[512,512]{1,0:T(8,128)(2,1)}, u32[]{:S(2)}) copy-start(bf16[512,512]{1,0:T(8,128)(2,1)} %param.8) | copy-start | bytes 1572868
  7.2 119.6 %all-gather.3.cloned.1.call-start = ((), (), s32[]{:S(2)}) async-start(), calls=%async_computation.2 | async-start | bytes 1769472 | tf_op jit(solution)/shard_map/all_gather | solution.py:26
  7.9 206.0 %reduce-scatter.3.cloned.1.call-start = ((), (), s32[]{:S(2)}) async-start(), calls=%async_computation.3 | async-start | bytes 3342336 | tf_op jit(solution)/shard_map/reduce_scatter | solution.py:31
  17.0 10.0 %copy-start.1 = (s32[1,1,2,288]{3,2,1,0:T(2,128)S(1)}, s32[1,1,2,288]{3,2,1,0:T(2,128)}, u32[]{:S(2)}) copy-start(s32[1,1,2,288]{3,2,1,0:T(2,128)} %param.10) | copy-start | bytes 6916
  136.1 79.9 %copy-start.2 = (bf16[192,512]{1,0:T(8,128)(2,1)S(1)}, bf16[192,512]{1,0:T(8,128)(2,1)}, u32[]{:S(2)}) copy-start(bf16[192,512]{1,0:T(8,128)(2,1)} %param.7) | copy-start | bytes 589828
  136.1 132.2 %all-gather.5.cloned.1.call-start = ((), (), s32[]{:S(2)}) async-start(), calls=%async_computation.5 | async-start | bytes 3342336 | tf_op jit(solution)/shard_map/all_gather | solution.py:44
  213.9 3.1 copy-start.3
  217.0 202.0 %all-reduce.2.cloned.1.call-start = ((), (), s32[]{:S(2)}) async-start(), calls=%async_computation.4 | async-start | bytes 2097152 | tf_op jit(solution)/shard_map/psum | solution.py:49
  218.5 243.9 %reduce-scatter.5.cloned.1.call-start = ((), (), s32[]{:S(2)}) async-start(), calls=%async_computation.6 | async-start | bytes 1769472 | tf_op jit(solution)/shard_map/reduce_scatter | solution.py:55
Sparse Core Ops, SparseCore 0:
  9.7 43.1 all-gather.2
  136.2 77.6 reduce-scatter.2
  217.1 51.1 all-gather.4
  273.5 145.4 all-reduce.1
  422.0 40.3 reduce-scatter.4
where the time goes:
time: 471 us; the launch traced here: 469 us
  waiting for transfers between devices  309 us (66%)
  local copies, waits for them, and re-layouts  68.8 us (15%)
  other arithmetic  51.7 us (11%)
  matrix products  24.1 us (5%)
  between operations  14.5 us (3%)
    psum x1, waiting for transfers between devices, per_device(): lax.psum(local_wgrad, ('row', 'col'))  140 us
    reduce_scatter x1, waiting for transfers between devices, per_device(): lax.psum_scatter(partial_agg.astype(jnp.bfloat16), 'col', scatter_dimensi...  77.8 us
    all_gather x1, waiting for transfers between devices, per_device(): grad_rows = lax.all_gather(grad_agg, 'col', axis=0, tiled=True)  49.6 us
    scatter-add x1, other arithmetic, per_device(): dense_tile = dense_tile.at[row_ids, :, col_ids, :].add(slot_vals)  45.5 us
    reduce_scatter x1, waiting for transfers between devices, per_device(): lax.psum_scatter(partial_grad.astype(jnp.bfloat16), 'row', scatter_dimens...  41 us
    reshape x1, local copies, waits for them, and re-layouts, per_device(): dense_tile = dense_tile.reshape(block_rows * side, block_cols * side)  24.6 us
    scatter-add x1, local copies, waits for them, and re-layouts, per_device(): dense_tile = dense_tile.at[row_ids, :, col_ids, :].add(slot_vals)  22.7 us
    dot_general x1, matrix products, per_device(): lax.dot_general(dense_tile, grad_rows, (((0,), (0,)), ((), ())), preferre...  10.4 us
  transfers between devices with their start and end apart: 5, of which 4 were waited for; matrix products, arithmetic and copies ran while one was open for 28% of the time, Pallas kernels for 0%

commit v1 on v0

--- a/solution.py
+++ b/solution.py
@@ -41,7 +41,8 @@
     grad_agg = lax.dot_general(
         grad_pre, weight, (((1,), (1,)), ((), ())), preferred_element_type=jnp.float32
     ).astype(jnp.bfloat16)
-    grad_rows = lax.all_gather(grad_agg, "col", axis=0, tiled=True)
+    sent = jnp.stack([grad_agg] * lax.axis_size("col"))
+    grad_rows = jnp.concatenate(lax.all_to_all(sent, "col", 0, 0), axis=0)
     local_wgrad = lax.dot_general(
         aggregated, grad_pre, (((0,), (0,)), ((), ())), preferred_element_type=jnp.float32
     )

time: 471 us -> 444 us (0.943)
  waiting for transfers between devices: 309 us -> 277 us
    all_gather x1 -> x0, waiting for transfers between devices: 49.6 us -> none  [per_device(): grad_rows = lax.all_gather(grad_agg, 'col', axis=0, tiled=True)]
    all_to_all x0 -> x1, waiting for transfers between devices: none -> 40.9 us  [per_device(): grad_rows = jnp.concatenate(lax.all_to_all(sent, 'col', 0, 0), axis=0)]
    psum x1, waiting for transfers between devices: 140 us -> 116 us  [per_device(): lax.psum(local_wgrad, ('row', 'col'))]
  transfers between devices with their start and end apart: 5 -> 5, of which waited for: 4 -> 4; matrix products, arithmetic and copies ran while one was open for 28% -> 30% of each run, Pallas kernels for 0% -> 0%
where the time goes in v1:
time: 444 us; the launch traced here: 442 us
  waiting for transfers between devices  277 us (62%)
  local copies, waits for them, and re-layouts  70.7 us (16%)
  other arithmetic  51.7 us (12%)
  matrix products  23.4 us (5%)
  between operations  14.5 us (3%)
  starting transfers between devices  4.96 us (1%)
    psum x1, waiting for transfers between devices, per_device(): lax.psum(local_wgrad, ('row', 'col'))  116 us
    reduce_scatter x1, waiting for transfers between devices, per_device(): lax.psum_scatter(partial_agg.astype(jnp.bfloat16), 'col', scatter_dimensi...  77.9 us
    scatter-add x1, other arithmetic, per_device(): dense_tile = dense_tile.at[row_ids, :, col_ids, :].add(slot_vals)  45.6 us
    reduce_scatter x1, waiting for transfers between devices, per_device(): lax.psum_scatter(partial_grad.astype(jnp.bfloat16), 'row', scatter_dimens...  41 us
    all_to_all x1, waiting for transfers between devices, per_device(): grad_rows = jnp.concatenate(lax.all_to_all(sent, 'col', 0, 0), axis=0)  40.9 us
    reshape x1, local copies, waits for them, and re-layouts, per_device(): dense_tile = dense_tile.reshape(block_rows * side, block_cols * side)  24.6 us
    scatter-add x1, local copies, waits for them, and re-layouts, per_device(): dense_tile = dense_tile.at[row_ids, :, col_ids, :].add(slot_vals)  22.7 us
    dot_general x1, matrix products, per_device(): lax.dot_general(dense_tile, grad_rows, (((0,), (0,)), ((), ())), preferre...  10.5 us
  transfers between devices with their start and end apart: 5, of which 4 were waited for; matrix products, arithmetic and copies ran while one was open for 30% of the time, Pallas kernels for 0%

profile of v1, /device:TPU:0, one launch (start us, length us, event | category | flops | bytes accessed | tf_op | source)
XLA Modules:
  0.0 441.9 jit_solution(3526511494331733221)
XLA Ops:
  7.2 0.0 copy-start
  7.2 0.0 all-gather.2.cloned.1.call-start
  7.2 0.7 all-gather.2.cloned.1.call-update
  7.9 0.0 reduce-scatter.3.cloned.1.call-start
  8.0 4.5 %copy.9 = bf16[1,1,288,4096]{2,3,1,0:T(8,128)(2,1)} copy(bf16[1,1,288,4096]{3,2,1,0:T(8,128)(2,1)} %param.9) | data formatting | bytes 4718592 | tf_op args[3]
  13.1 3.8 broadcast_select_fusion
  17.0 0.0 copy-start.1
  17.0 9.9 %copy.10 = bf16[288,64,64]{2,1,0:T(8,128)(2,1)} copy(bf16[288,64,64]{0,2,1:T(8,128)(2,1)} %broadcast_select_fusion) | data formatting | bytes 4718592 | tf_op jit(solution)/shard_map/jit(_where)/select_n | solution.py:25
  26.9 0.0 copy-done.1
  26.9 7.0 %broadcast_in_dim.17 = bf16[48,64,24,64]{3,1,2,0:T(8,128)(2,1)} broadcast(bf16[]{:T(256)} %constant.6.clone.1), dimensions={} | broadcast | bytes 9437186 | tf_op jit(solution)/shard_map/broadcast_in_dim | solution.py:27
  33.9 45.6 %scatter_fusion = bf16[48,64,24,64]{3,1,2,0:T(8,128)(2,1)} fusion(bf16[48,64,24,64]{3,1,2,0:T(8,128)(2,1)} %broadcast_in_dim.17, s32[288]{0:T(512)S(1)} %fusion.1, bf16[288,64,64]{2,1,0:T(8,128)(2,1)} %copy.10), kind=kCustom, calls=%fused_computation | custom fusion | flops 1179648 | bytes 7080192 | tf_op jit(solution)/shard_map/scatter-add | solution.py:28
  79.5 22.7 %copy.11 = bf16[48,64,24,64]{3,2,1,0:T(8,128)(2,1)} copy(bf16[48,64,24,64]{3,1,2,0:T(8,128)(2,1)} %scatter_fusion) | data formatting | bytes 18874368 | tf_op jit(solution)/shard_map/scatter-add | solution.py:28
  102.2 24.6 %reshape.78 = bf16[3072,1536]{1,0:T(8,128)(2,1)} reshape(bf16[48,64,24,64]{3,2,1,0:T(8,128)(2,1)} %copy.11) | data formatting | bytes 18874368 | tf_op jit(solution)/shard_map/reshape | solution.py:29
  126.8 0.0 all-gather.2.cloned.1.call-done
  126.8 9.2 %convolution_convert_fusion = bf16[3072,512]{1,0:T(8,128)(2,1)} fusion(bf16[3072,1536]{1,0:T(8,128)(2,1)} %reshape.78, bf16[1536,512]{1,0:T(8,128)(2,1)} %all-gather.2.cloned.1.call-done), kind=kOutput, calls=%fused_computation.1 | convolution fusion | flops 4833411072 | bytes 14155776 | tf_op jit(solution)/shard_map/dot_general | solution.py:30
  136.0 0.0 copy-start.2
  136.0 0.0 reduce-scatter.3.cloned.1.call-update
  136.1 77.9 %reduce-scatter.3.cloned.1.call-done = bf16[192,512]{1,0:T(8,128)(2,1)} async-done(((bf16[3072,512]{1,0:T(8,128)(2,1)}), bf16[192,512]{1,0:T(8,128)(2,1)}) %reduce-scatter.3.cloned.1.call-update) | async-done | bytes 196624 | tf_op jit(solution)/shard_map/reduce_scatter | solution.py:31
  213.9 0.0 copy-done
  213.9 1.9 multiply_convert_fusion.1
  215.9 0.0 copy-done.2
  215.9 0.3 convolution_convert_fusion.2
  216.2 2.0 stack.2
  218.2 0.0 copy-start.3
  218.2 4.6 %all-to-all-start = ((bf16[16,192,512]{2,1,0:T(8,128)(2,1)}), bf16[16,192,512]{2,1,0:T(8,128)(2,1)}, u32[]{:S(2)}, u32[]{:S(2)}) async-start(bf16[16,192,512]{2,1,0:T(8,128)(2,1)} %stack.2), calls=%async_computation.1 | async-start | bytes 6291456 | tf_op jit(solution)/shard_map/all_to_all | solution.py:45
  222.8 0.0 all-reduce.2.cloned.1.call-start
  222.8 0.0 copy-done.3
  222.8 1.4 fusion.2
  224.3 0.0 all-reduce.2.cloned.1.call-update
  224.3 0.2 reduce-scatter.5.cloned.1.call-start
  224.5 40.9 %all-to-all-done = bf16[16,192,512]{2,1,0:T(8,128)(2,1)} async-done(((bf16[16,192,512]{2,1,0:T(8,128)(2,1)}), bf16[16,192,512]{2,1,0:T(8,128)(2,1)}, u32[]{:S(2)}, u32[]{:S(2)}) %all-to-all-start) | async-done | bytes 3145760 | tf_op jit(solution)/shard_map/all_to_all | solution.py:45
  265.4 10.5 %convolution_convert_fusion.1 = bf16[1536,512]{1,0:T(8,128)(2,1)} fusion(bf16[3072,1536]{1,0:T(8,128)(2,1)} %reshape.78, bf16[3072,512]{1,0:T(8,128)(2,1)} %bitcast.4), kind=kOutput, calls=%fused_computation.3 | convolution fusion | flops 4832624640 | bytes 14155776 | tf_op jit(solution)/shard_map/dot_general | solution.py:52
  275.8 0.0 reduce-scatter.5.cloned.1.call-update
  275.8 116.2 %all-reduce.2.cloned.1.call-done = f32[512,512]{1,0:T(8,128)} async-done(((f32[512,512]{1,0:T(8,128)}), f32[512,512]{1,0:T(8,128)}) %all-reduce.2.cloned.1.call-update) | async-done | bytes 1048592 | tf_op jit(solution)/shard_map/psum | solution.py:50
  392.1 2.3 broadcast_multiply_fusion
  394.4 41.0 %reduce-scatter.5.cloned.1.call-done = bf16[192,512]{1,0:T(8,128)(2,1)} async-done(((bf16[1536,512]{1,0:T(8,128)(2,1)}), bf16[192,512]{1,0:T(8,128)(2,1)}) %reduce-scatter.5.cloned.1.call-update) | async-done | bytes 196624 | tf_op jit(solution)/shard_map/reduce_scatter | solution.py:56
  (2 shorter events, 0.0 us)
Async XLA Ops:
  7.2 206.8 %copy-start = (bf16[512,512]{1,0:T(8,128)(2,1)S(1)}, bf16[512,512]{1,0:T(8,128)(2,1)}, u32[]{:S(2)}) copy-start(bf16[512,512]{1,0:T(8,128)(2,1)} %param.8) | copy-start | bytes 1572868
  7.2 119.6 %all-gather.2.cloned.1.call-start = ((), (), s32[]{:S(2)}) async-start(), calls=%async_computation.3 | async-start | bytes 1769472 | tf_op jit(solution)/shard_map/all_gather | solution.py:26
  7.9 206.0 %reduce-scatter.3.cloned.1.call-start = ((), (), s32[]{:S(2)}) async-start(), calls=%async_computation.4 | async-start | bytes 3342336 | tf_op jit(solution)/shard_map/reduce_scatter | solution.py:31
  17.0 9.9 %copy-start.1 = (s32[1,1,2,288]{3,2,1,0:T(2,128)S(1)}, s32[1,1,2,288]{3,2,1,0:T(2,128)}, u32[]{:S(2)}) copy-start(s32[1,1,2,288]{3,2,1,0:T(2,128)} %param.10) | copy-start | bytes 6916
  136.0 79.8 %copy-start.2 = (bf16[192,512]{1,0:T(8,128)(2,1)S(1)}, bf16[192,512]{1,0:T(8,128)(2,1)}, u32[]{:S(2)}) copy-start(bf16[192,512]{1,0:T(8,128)(2,1)} %param.7) | copy-start | bytes 589828
  218.2 4.7 %copy-start.3 = (bf16[192,512]{1,0:T(8,128)(2,1)S(1)}, bf16[192,512]{1,0:T(8,128)(2,1)}, u32[]{:S(2)}) copy-start(bf16[192,512]{1,0:T(8,128)(2,1)} %reduce-scatter.3.cloned.1.call-done) | copy-start | bytes 589828
  218.2 47.2 %all-to-all-start = ((bf16[16,192,512]{2,1,0:T(8,128)(2,1)}), bf16[16,192,512]{2,1,0:T(8,128)(2,1)}, u32[]{:S(2)}, u32[]{:S(2)}) async-start(bf16[16,192,512]{2,1,0:T(8,128)(2,1)} %stack.2), calls=%async_computation.1 | async-start | bytes 6291456 | tf_op jit(solution)/shard_map/all_to_all | solution.py:45
  222.8 169.3 %all-reduce.2.cloned.1.call-start = ((), (), s32[]{:S(2)}) async-start(), calls=%async_computation.5 | async-start | bytes 2097152 | tf_op jit(solution)/shard_map/psum | solution.py:50
  224.3 211.1 %reduce-scatter.5.cloned.1.call-start = ((), (), s32[]{:S(2)}) async-start(), calls=%async_computation.6 | async-start | bytes 1769472 | tf_op jit(solution)/shard_map/reduce_scatter | solution.py:56
Sparse Core Ops, SparseCore 0:
  9.7 43.1 all-gather.1
  136.2 77.6 reduce-scatter.2
  229.0 163.0 all-reduce.1
  395.0 40.3 reduce-scatter.4
